TPU v7x, 128 devices: a whole 4x4x4 slice. The times are simulated.
128 devices in a mesh: ta: 8 (over z, core), af: 16 (over x, y).
Axes of the slice: x: 4, y: 4, z: 4, core: 2. Of those that a mesh axis runs over, the one named last changes fastest.
Arguments:
- velocity: float32 [16, 512, 128, 128], P(None, ('ta', 'af')), may hold values from -14 to 14
- initial_basis: float32 [512, 64], replicated, may hold values from -6 to 6
Outputs:
- core: float32 [16, 128, 64, 128], P('ta', 'af')
All inputs are finite; a program needn't handle non-finite values.
Results may differ from a plain program's by a relative error of at most 0.00017.
Values sent between devices are 32-bit elements; how exact they have to be, the bound alone decides.
A program may use at most 64 MiB of HBM per device.

v0:
```python
import jax
import jax.numpy as jnp
from jax import lax
from jax.sharding import PartitionSpec as P

ITERS = 3


def orthonormal(product):
    lower = jnp.linalg.cholesky(
        jnp.dot(
            product.T, product, precision=lax.Precision.HIGHEST, preferred_element_type=jnp.float32
        )
    )
    return jax.scipy.linalg.solve_triangular(lower, product.T, lower=True).T


def local(velocity, initial_basis):
    groups_ta = lax.axis_size("ta")
    groups_af = lax.axis_size("af")
    frames, slab_planes, cells_x, cells_y = velocity.shape
    planes_total = initial_basis.shape[0]
    blocked = velocity.reshape(
        groups_ta, frames // groups_ta, slab_planes, groups_af, cells_x // groups_af, cells_y
    )
    blocked = blocked.transpose(0, 3, 1, 2, 4, 5).reshape(
        groups_ta * groups_af, frames // groups_ta, slab_planes, cells_x // groups_af, cells_y
    )
    fibres = lax.all_to_all(blocked, ("ta", "af"), split_axis=0, concat_axis=2, tiled=True)
    fibres = fibres.reshape(frames // groups_ta, planes_total, cells_x // groups_af, cells_y)
    gram_local = jnp.einsum(
        "fzxy,fwxy->zw",
        fibres,
        fibres,
        precision=lax.Precision.HIGHEST,
        preferred_element_type=jnp.float32,
    )
    gram_matrix = lax.psum(gram_local, ("ta", "af"))
    subspace = initial_basis
    for iteration in range(ITERS):
        subspace = orthonormal(
            jnp.dot(
                gram_matrix,
                subspace,
                precision=lax.Precision.HIGHEST,
                preferred_element_type=jnp.float32,
            )
        )
    return jnp.einsum(
        "fzxy,zk->fxky",
        fibres,
        subspace,
        precision=lax.Precision.HIGHEST,
        preferred_element_type=jnp.float32,
    )


def solution(mesh):
    placed = (P(None, ("ta", "af"), None, None), P())
    return jax.shard_map(
        local, mesh=mesh, in_specs=placed, out_specs=P("ta", "af", None, None), check_vma=False
    )
```

profile of v0, /device:TPU:1, one launch (start us, length us, event | category | flops | bytes accessed | tf_op | source)
XLA Modules:
  0.0 287.6 jit_solution(15660621444785246462)
XLA Ops:
  6.5 5.0 %copy.7 = f32[8,2,4,16,8,128]{5,2,4,1,3,0:T(4,128)S(1)} copy(f32[8,2,4,16,8,128]{5,4,3,2,1,0:T(8,128)} %bitcast.74) | data formatting | bytes 8388608 | tf_op jit(solution)/shard_map/reshape | solution.py:23
  11.5 64.0 %all_to_all.15 = f32[128,2,4,8,128]{4,2,3,1,0:T(4,128)S(1)} all-to-all(f32[128,2,4,8,128]{4,2,3,1,0:T(4,128)S(1)} %bitcast.73), channel_id=1, replica_groups=mesh['ta'=8,'af'=16] {'ta','af'}, dimensions={0} | all-to-all | bytes 8388608 | tf_op jit(solution)/shard_map/all_to_all | solution.py:29
  75.5 1.0 copy.8
  76.5 1.9 copy-done.1
  78.4 7.9 %convolution_bitcast_fusion = f32[512,512]{1,0:T(8,128)} fusion(f32[2,512,8,128]{3,1,2,0:T(8,128)S(1)} %bitcast.70), kind=kOutput, calls=%fused_computation | convolution fusion | flops 6442450944 | bytes 5242880 | tf_op jit(solution)/shard_map/fzxy,fwxy->zw/dot_general | solution.py:31
  86.3 144.4 %all-reduce.2.cloned.1.call-done = f32[512,512]{1,0:T(8,128)} async-done(((f32[512,512]{1,0:T(8,128)}), f32[512,512]{1,0:T(8,128)}) %all-reduce.2.cloned.1.call-update) | async-done | bytes 1048592 | tf_op jit(solution)/shard_map/psum | solution.py:38
  230.7 2.4 fusion.18
  233.5 5.8 %cholesky.59 = f32[64,64]{1,0:T(8,128)S(1)} custom-call(f32[64,64]{1,0:T(8,128)S(1)} %fusion.13), custom_call_target="Cholesky" | custom-call | tf_op jit(solution)/shard_map/jit(cholesky)/cholesky | solution.py:10
  239.4 0.6 compare_reduce_fusion.2
  240.1 0.7 fusion.5
  240.7 4.9 %custom-call.7 = f32[1,64,64]{1,2,0:T(8,128)S(1)} custom-call(f32[1,64,64]{2,1,0:T(8,128)S(1)} %fusion.5), custom_call_target="InvertDiagBlocksLowerTriangular" | custom-call | tf_op jit(solution)/shard_map/jit(_solve_triangular)/triangular_solve | solution.py:15
  245.6 0.3 fusion.3
  246.0 2.4 fusion.20
  248.7 6.0 %cholesky.70 = f32[64,64]{1,0:T(8,128)S(1)} custom-call(f32[64,64]{1,0:T(8,128)S(1)} %fusion.11), custom_call_target="Cholesky" | custom-call | tf_op jit(solution)/shard_map/jit(cholesky)/cholesky | solution.py:10
  254.7 0.6 compare_reduce_fusion.1
  255.4 0.7 fusion.6
  256.0 4.9 %custom-call.8 = f32[1,64,64]{1,2,0:T(8,128)S(1)} custom-call(f32[1,64,64]{2,1,0:T(8,128)S(1)} %fusion.6), custom_call_target="InvertDiagBlocksLowerTriangular" | custom-call | tf_op jit(solution)/shard_map/jit(_solve_triangular)/triangular_solve | solution.py:15
  261.3 1.1 fusion.22
  262.8 5.8 %cholesky.81 = f32[64,64]{1,0:T(8,128)S(1)} custom-call(f32[64,64]{1,0:T(8,128)S(1)} %fusion.9), custom_call_target="Cholesky" | custom-call | tf_op jit(solution)/shard_map/jit(cholesky)/cholesky | solution.py:10
  268.6 0.6 compare_reduce_fusion
  269.3 0.7 fusion.7
  269.9 4.9 %custom-call.9 = f32[1,64,64]{1,2,0:T(8,128)S(1)} custom-call(f32[1,64,64]{2,1,0:T(8,128)S(1)} %fusion.7), custom_call_target="InvertDiagBlocksLowerTriangular" | custom-call | tf_op jit(solution)/shard_map/jit(_solve_triangular)/triangular_solve | solution.py:15
  274.8 0.3 convolution_bitcast_fusion.2
  275.2 5.6 %convolution_bitcast_fusion.1 = f32[2,8,64,128]{3,2,1,0:T(8,128)} fusion(f32[64,512,1,1]{1,0,3,2:T(8,128)S(1)} %convolution_bitcast_fusion.2, f32[2,512,8,128]{3,1,2,0:T(8,128)} %bitcast.71), kind=kOutput, calls=%fused_computation.1 | convolution fusion | flops 805306368 | bytes 4849664 | tf_op jit(solution)/shard_map/fzxy,zk->fxky/dot_general | solution.py:49
  (20 shorter events, 1.5 us)
Async XLA Ops:
  6.5 224.2 %copy-start = (f32[512,64]{0,1:T(8,128)S(1)}, f32[512,64]{0,1:T(8,128)}, u32[]{:S(2)}) copy-start(f32[512,64]{0,1:T(8,128)} %param.6) | copy-start | bytes 393220
  6.5 224.2 %all-reduce.2.cloned.1.call-start = ((), (), s32[]{:S(2)}) async-start(), calls=%async_computation.1 | async-start | bytes 2097152 | tf_op jit(solution)/shard_map/psum | solution.py:38
  76.5 1.9 copy-start.1
  230.7 30.5 %copy-start.2 = (f32[512,512]{1,0:T(8,128)S(1)}, f32[512,512]{1,0:T(8,128)}, u32[]{:S(2)}) copy-start(f32[512,512]{1,0:T(8,128)} %all-reduce.2.cloned.1.call-done) | copy-start | bytes 3145732
Sparse Core Ops, SparseCore 0:
  86.5 144.2 all-reduce.1
where the time goes:
time: 288 us
  waiting for transfers between devices  144 us (50%)
  blocking collectives  64 us (22%)
  other arithmetic  36.4 us (13%)
  matrix products  21.3 us (7%)
  between operations  13.5 us (5%)
  local copies, waits for them, and re-layouts  8.09 us (3%)
    psum x1, waiting for transfers between devices, local(): gram_matrix = lax.psum(gram_local, ('ta', 'af'))  144 us
    all_to_all x1, blocking collectives, local(): lax.all_to_all(blocked, ('ta', 'af'), split_axis=0, concat_axis=2, tiled=...  64 us
    another operation x9, other arithmetic, orthonormal(): jnp.linalg.cholesky(jnp.dot(product.T, product, precision=lax.Precision.H...  19.7 us
    another operation x6, other arithmetic, orthonormal(): return jax.scipy.linalg.solve_triangular(lower, product.T, lower=True).T  16.6 us
    dot_general x1, matrix products, local(): jnp.einsum('fzxy,fwxy->zw', fibres, fibres, precision=lax.Precision.HIGHE...  7.93 us
    dot_general x3, matrix products, local(): jnp.dot(gram_matrix, subspace, precision=lax.Precision.HIGHEST, preferred...  5.94 us
  transfers between devices with their start and end apart: 1, of which 1 were waited for; matrix products, arithmetic and copies ran while one was open for 0% of the time, Pallas kernels for 0%

commit v1 on v0

--- a/solution.py
+++ b/solution.py
@@ -26,7 +26,12 @@
     blocked = blocked.transpose(0, 3, 1, 2, 4, 5).reshape(
         groups_ta * groups_af, frames // groups_ta, slab_planes, cells_x // groups_af, cells_y
     )
-    fibres = lax.all_to_all(blocked, ("ta", "af"), split_axis=0, concat_axis=2, tiled=True)
+    fibres = jnp.concatenate(
+        lax.all_to_all(
+            jnp.stack(jnp.split(blocked, lax.axis_size(("ta", "af")), axis=0)), ("ta", "af"), 0, 0
+        ),
+        axis=2,
+    )
     fibres = fibres.reshape(frames // groups_ta, planes_total, cells_x // groups_af, cells_y)
     gram_local = jnp.einsum(
         "fzxy,fwxy->zw",

time: 288 us -> 290 us (level)
  no operation moved by 1% of the time
where the time goes in v1:
time: 290 us
  waiting for transfers between devices  144 us (50%)
  blocking collectives  64 us (22%)
  other arithmetic  36.4 us (13%)
  matrix products  21.3 us (7%)
  between operations  14.1 us (5%)
  local copies, waits for them, and re-layouts  9.5 us (3%)
    psum x1, waiting for transfers between devices, local(): gram_matrix = lax.psum(gram_local, ('ta', 'af'))  144 us
    all_to_all x1, blocking collectives, local(): lax.all_to_all(jnp.stack(jnp.split(blocked, lax.axis_size(('ta', 'af')),...  64 us
    another operation x9, other arithmetic, orthonormal(): jnp.linalg.cholesky(jnp.dot(product.T, product, precision=lax.Precision.H...  19.7 us
    another operation x6, other arithmetic, orthonormal(): return jax.scipy.linalg.solve_triangular(lower, product.T, lower=True).T  16.6 us
    dot_general x1, matrix products, local(): jnp.einsum('fzxy,fwxy->zw', fibres, fibres, precision=lax.Precision.HIGHE...  7.93 us
    dot_general x3, matrix products, local(): jnp.dot(gram_matrix, subspace, precision=lax.Precision.HIGHEST, preferred...  5.94 us
  transfers between devices with their start and end apart: 1, of which 1 were waited for; matrix products, arithmetic and copies ran while one was open for 0% of the time, Pallas kernels for 0%

profile of v1, /device:TPU:1, one launch (start us, length us, event | category | flops | bytes accessed | tf_op | source)
XLA Modules:
  0.0 289.7 jit_solution(6423642127720284553)
XLA Ops:
  6.5 5.0 %copy.134 = f32[8,2,4,16,8,128]{5,2,4,1,3,0:T(4,128)S(1)} copy(f32[8,2,4,16,8,128]{5,4,3,2,1,0:T(8,128)} %bitcast.711) | data formatting | bytes 8388608 | tf_op jit(solution)/shard_map/reshape | solution.py:23
  13.5 64.0 %all_to_all.5 = f32[128,1,2,4,8,128]{5,3,4,2,1,0:T(4,128)S(1)} all-to-all(f32[128,1,2,4,8,128]{5,3,4,2,1,0:T(4,128)S(1)} %constant_dynamic-update-slice_fusion), channel_id=1, replica_groups=mesh['ta'=8,'af'=16] {'ta','af'}, dimensions={0} | all-to-all | bytes 8388608 | tf_op jit(solution)/shard_map/all_to_all | solution.py:30
  77.5 1.0 copy.135
  78.5 1.9 copy-done.1
  80.4 7.9 %convolution_bitcast_fusion = f32[512,512]{1,0:T(8,128)} fusion(f32[2,512,8,128]{3,1,2,0:T(8,128)S(1)} %bitcast.580), kind=kOutput, calls=%fused_computation | convolution fusion | flops 6442450944 | bytes 5242880 | tf_op jit(solution)/shard_map/fzxy,fwxy->zw/dot_general | solution.py:36
  88.4 144.4 %all-reduce.2.cloned.1.call-done = f32[512,512]{1,0:T(8,128)} async-done(((f32[512,512]{1,0:T(8,128)}), f32[512,512]{1,0:T(8,128)}) %all-reduce.2.cloned.1.call-update) | async-done | bytes 1048592 | tf_op jit(solution)/shard_map/psum | solution.py:43
  232.7 2.4 fusion.18
  235.6 5.8 %cholesky.59 = f32[64,64]{1,0:T(8,128)S(1)} custom-call(f32[64,64]{1,0:T(8,128)S(1)} %fusion.13), custom_call_target="Cholesky" | custom-call | tf_op jit(solution)/shard_map/jit(cholesky)/cholesky | solution.py:10
  241.4 0.6 compare_reduce_fusion.2
  242.1 0.7 fusion.5
  242.7 4.9 %custom-call.7 = f32[1,64,64]{1,2,0:T(8,128)S(1)} custom-call(f32[1,64,64]{2,1,0:T(8,128)S(1)} %fusion.5), custom_call_target="InvertDiagBlocksLowerTriangular" | custom-call | tf_op jit(solution)/shard_map/jit(_solve_triangular)/triangular_solve | solution.py:15
  247.6 0.3 fusion.3
  248.0 2.4 fusion.20
  250.7 6.0 %cholesky.70 = f32[64,64]{1,0:T(8,128)S(1)} custom-call(f32[64,64]{1,0:T(8,128)S(1)} %fusion.11), custom_call_target="Cholesky" | custom-call | tf_op jit(solution)/shard_map/jit(cholesky)/cholesky | solution.py:10
  256.7 0.6 compare_reduce_fusion.1
  257.4 0.7 fusion.6
  258.0 4.9 %custom-call.8 = f32[1,64,64]{1,2,0:T(8,128)S(1)} custom-call(f32[1,64,64]{2,1,0:T(8,128)S(1)} %fusion.6), custom_call_target="InvertDiagBlocksLowerTriangular" | custom-call | tf_op jit(solution)/shard_map/jit(_solve_triangular)/triangular_solve | solution.py:15
  263.3 1.1 fusion.22
  264.8 5.8 %cholesky.81 = f32[64,64]{1,0:T(8,128)S(1)} custom-call(f32[64,64]{1,0:T(8,128)S(1)} %fusion.9), custom_call_target="Cholesky" | custom-call | tf_op jit(solution)/shard_map/jit(cholesky)/cholesky | solution.py:10
  270.7 0.6 compare_reduce_fusion
  271.3 0.7 fusion.7
  272.0 4.9 %custom-call.9 = f32[1,64,64]{1,2,0:T(8,128)S(1)} custom-call(f32[1,64,64]{2,1,0:T(8,128)S(1)} %fusion.7), custom_call_target="InvertDiagBlocksLowerTriangular" | custom-call | tf_op jit(solution)/shard_map/jit(_solve_triangular)/triangular_solve | solution.py:15
  276.9 0.3 convolution_bitcast_fusion.2
  277.2 5.6 %convolution_bitcast_fusion.1 = f32[2,8,64,128]{3,2,1,0:T(8,128)} fusion(f32[64,512,1,1]{1,0,3,2:T(8,128)S(1)} %convolution_bitcast_fusion.2, f32[2,512,8,128]{3,1,2,0:T(8,128)} %bitcast.581), kind=kOutput, calls=%fused_computation.1 | convolution fusion | flops 805306368 | bytes 4849664 | tf_op jit(solution)/shard_map/fzxy,zk->fxky/dot_general | solution.py:54
  (148 shorter events, 2.9 us)
Async XLA Ops:
  6.5 226.2 %copy-start = (f32[512,64]{0,1:T(8,128)S(1)}, f32[512,64]{0,1:T(8,128)}, u32[]{:S(2)}) copy-start(f32[512,64]{0,1:T(8,128)} %param.6) | copy-start | bytes 393220
  6.5 226.2 %all-reduce.2.cloned.1.call-start = ((), (), s32[]{:S(2)}) async-start(), calls=%async_computation.1 | async-start | bytes 2097152 | tf_op jit(solution)/shard_map/psum | solution.py:43
  78.5 1.9 copy-start.1
  232.7 30.5 %copy-start.2 = (f32[512,512]{1,0:T(8,128)S(1)}, f32[512,512]{1,0:T(8,128)}, u32[]{:S(2)}) copy-start(f32[512,512]{1,0:T(8,128)} %all-reduce.2.cloned.1.call-done) | copy-start | bytes 3145732
Sparse Core Ops, SparseCore 0:
  88.5 144.2 all-reduce.1
